TPU v7x, 32 devices: a whole 2x2x4 slice. The times are simulated.
32 devices in a mesh: ra: 16 (over z, x, core), freq: 2 (over y).
Axes of the slice: x: 2, y: 2, z: 4, core: 2. Of those that a mesh axis runs over, the one named last changes fastest.
Arguments:
- solution: float32 [1920, 2048], P('freq', 'ra'), may hold values from -6 to 6
- residual: float32 [1920, 2048], P('freq', 'ra'), may hold values from -20 to 20
- direction: float32 [1920, 2048], P('freq', 'ra'), may hold values from -20 to 20
- sidereal: float32 [64], P('ra'), may hold values from -3.140625 to 3.140625
- response: float32 [64, 640], P('ra'), may hold values from 0.03 to 0.3
- significant: int32 [64, 10], P('ra'), may hold values from 0 to 1, as said below
- inv_noise: float32 [64, 1920], P('ra', 'freq'), may hold values from 0.25 to 4
Outputs:
- solution_next: float32 [1920, 2048], P('freq', 'ra')
- residual_next: float32 [1920, 2048], P('freq', 'ra')
- direction_next: float32 [1920, 2048], P('freq', 'ra')
Inputs may be any that keep to these rules, and one draw needn't show every extreme that they name: `significant`: the ones of a row form one run of consecutive columns.
All inputs are finite; a program needn't handle non-finite values.
Results may differ from a plain program's by a relative error of at most 0.0003.
Values sent between devices are 32-bit elements; how exact they have to be, the bound alone decides.
A program may use at most 64 MiB of HBM per device.

v0:
```python
import jax
import jax.numpy as jnp
from jax import lax
from jax.sharding import PartitionSpec as P

NDEC = 64
RA_DEV = 2


TWO_PI = 6.283185307179586
HALF_TURN = 3.141592653589793
baseline_x = -0.006
baseline_y = 0.007
baseline_z = 0.0035
low_freq = 20.0
bin_width = 0.25
epsilon = 1e-06


def from_behind(value, axis, steps):
    count = lax.axis_size(axis)
    pairs = [(source, (source + steps) % count) for source in range(count)]
    return lax.ppermute(value, axis, pairs)


def pixel_angles(pixel_ids, columns):
    column = (pixel_ids // NDEC).astype(jnp.float32)
    dec_row = (pixel_ids % NDEC).astype(jnp.float32)
    right_asc = TWO_PI * (column + 0.5) / columns
    declin = HALF_TURN * ((dec_row + 0.5) / NDEC - 0.5)
    return (right_asc, declin)


def phase_tiles(sid_angle, weight, right_asc, declin, frequency):
    hour_angle = right_asc - sid_angle
    cos_dec = jnp.cos(declin)
    delays = (
        baseline_x * cos_dec * jnp.cos(hour_angle)
        + baseline_y * cos_dec * jnp.sin(hour_angle)
        + baseline_z * jnp.sin(declin)
    )
    phases = (TWO_PI * frequency)[:, None] * delays[None, :]
    return (weight[None, :] * jnp.cos(phases), weight[None, :] * jnp.sin(phases))


def pixel_weights(response, significant):
    return response * jnp.repeat(significant.astype(jnp.float32), NDEC, axis=1)


def segment_images(sid_angles, weights, noise_rows, window, right_asc, declin, frequency):

    def one_segment(running, segment_items):
        sid_angle, weight, noise_row = segment_items
        cos_tile, sin_tile = phase_tiles(sid_angle, weight, right_asc, declin, frequency)
        fwd_real = jnp.sum(cos_tile * window, axis=1)
        fwd_imag = jnp.sum(sin_tile * window, axis=1)
        return (
            running
            + cos_tile * (noise_row * fwd_real)[:, None]
            + sin_tile * (noise_row * fwd_imag)[:, None],
            None,
        )

    summed, _ = lax.scan(
        one_segment, jnp.zeros(window.shape, jnp.float32), (sid_angles, weights, noise_rows)
    )
    return summed


def shards(solution, residual, direction, sidereal, response, significant, inv_noise):
    cycle_size = lax.axis_size("ra")
    columns = RA_DEV * cycle_size
    block_id = lax.axis_index("ra")
    band_id = lax.axis_index("freq")
    freq_dev = direction.shape[0]
    pix_dev = direction.shape[1]
    frequency = low_freq + bin_width * (
        band_id * freq_dev + jnp.arange(freq_dev, dtype=jnp.int32)
    ).astype(jnp.float32)
    before = [direction]
    shifted = direction
    for offset in (1, 2):
        shifted = from_behind(shifted, "ra", 1)
        before.append(shifted)
    after = [direction]
    shifted = direction
    for offset in (1, 2):
        shifted = from_behind(shifted, "ra", -1)
        after.append(shifted)
    window = jnp.concatenate([before[2], before[1], direction, after[1], after[2]], axis=1)
    pixel_ids = jnp.mod(
        (block_id - 2) * pix_dev + jnp.arange(5 * pix_dev, dtype=jnp.int32), pix_dev * cycle_size
    )
    right_asc, declin = pixel_angles(pixel_ids, columns)
    summed = segment_images(
        sidereal,
        pixel_weights(response, significant),
        inv_noise,
        window,
        right_asc,
        declin,
        frequency,
    )
    pieces = [summed[:, part_id * pix_dev : (part_id + 1) * pix_dev] for part_id in range(5)]
    upward = jnp.zeros_like(direction)
    for part_id in (4, 3):
        upward = from_behind(upward + pieces[part_id], "ra", 1)
    downward = jnp.zeros_like(direction)
    for part_id in (0, 1):
        downward = from_behind(downward + pieces[part_id], "ra", -1)
    image = pieces[2] + upward + downward
    norm_raw, curvature, cross_term, image_norm = lax.psum(
        (
            jnp.sum(residual * residual),
            jnp.sum(direction * image),
            jnp.sum(residual * image),
            jnp.sum(image * image),
        ),
        ("ra", "freq"),
    )
    alpha = (norm_raw + epsilon) / (curvature + epsilon)
    solution_next = solution + alpha * direction
    residual_next = residual - alpha * image
    norm_next = norm_raw - 2.0 * alpha * cross_term + alpha * alpha * image_norm
    beta = norm_next / (norm_raw + epsilon)
    return (solution_next, residual_next, residual_next + beta * direction)


def solution(mesh):
    placed = (
        P("freq", "ra"),
        P("freq", "ra"),
        P("freq", "ra"),
        P("ra"),
        P("ra", None),
        P("ra", None),
        P("ra", "freq"),
    )
    return jax.shard_map(
        shards,
        mesh=mesh,
        in_specs=placed,
        out_specs=(P("freq", "ra"), P("freq", "ra"), P("freq", "ra")),
        check_vma=False,
    )
```

profile of v0, /device:TPU:0, one launch (start us, length us, event | category | flops | bytes accessed | tf_op | source)
XLA Modules:
  0.0 204.0 jit_solution(16120454747078484241)
XLA Ops:
  0.6 0.5 collective-permute-start
  1.2 5.0 %collective-permute-start.2 = (f32[960,128]{1,0:T(8,128)}, f32[960,128]{1,0:T(8,128)S(1)}, u32[]{:S(2)}, u32[]{:S(2)}) collective-permute-start(f32[960,128]{1,0:T(8,128)} %param.11), channel_id=1, source_target_pairs={{0,30},{2,0},{4,2},{6,4},{8,6},{10,8},{12,10},{14,12},{16,14},{18,... | collective-permute-start | bytes 1474568 | tf_op jit(solution)/shard_map/ppermute | solution.py:23
  6.2 6.8 %collective-permute-done = f32[960,128]{1,0:T(8,128)S(1)} collective-permute-done((f32[960,128]{1,0:T(8,128)}, f32[960,128]{1,0:T(8,128)S(1)}, u32[]{:S(2)}, u32[]{:S(2)}) %collective-permute-start) | collective-permute-done | bytes 491552 | tf_op jit(solution)/shard_map/ppermute | solution.py:23
  13.0 2.2 %collective-permute-start.1 = (f32[960,128]{1,0:T(8,128)S(1)}, f32[960,128]{1,0:T(8,128)}, u32[]{:S(2)}, u32[]{:S(2)}) collective-permute-start(f32[960,128]{1,0:T(8,128)S(1)} %collective-permute-done), channel_id=1, source_target_pairs={{0,2},{2,4},{4,6},{6,8},{8,10},{10,12},{12,14},{14,16},{16,18},{18... | collective-permute-start | bytes 1474568 | tf_op jit(solution)/shard_map/ppermute | solution.py:23
  15.1 0.7 convert_element_type.20
  15.8 0.1 broadcast_in_dim.5
  15.9 0.1 reshape.128
  16.0 0.7 mul.231
  16.7 0.0 copy-start.3
  16.7 0.0 collective-permute-done.2
  16.7 2.3 %collective-permute-start.3 = (f32[960,128]{1,0:T(8,128)S(1)}, f32[960,128]{1,0:T(8,128)S(1)}, u32[]{:S(2)}, u32[]{:S(2)}) collective-permute-start(f32[960,128]{1,0:T(8,128)S(1)} %collective-permute-done.2), channel_id=1, source_target_pairs={{0,30},{2,0},{4,2},{6,4},{8,6},{10,8},{12,10},{14,12},{16,14},{18,... | collective-permute-start | bytes 1474568 | tf_op jit(solution)/shard_map/ppermute | solution.py:23
  19.0 5.1 %collective-permute-done.1 = f32[960,128]{1,0:T(8,128)} collective-permute-done((f32[960,128]{1,0:T(8,128)S(1)}, f32[960,128]{1,0:T(8,128)}, u32[]{:S(2)}, u32[]{:S(2)}) %collective-permute-start.1) | collective-permute-done | bytes 491552 | tf_op jit(solution)/shard_map/ppermute | solution.py:23
  24.1 1.1 constant_dynamic-update-slice_fusion.4
  25.2 1.1 constant_dynamic-update-slice_fusion.2
  26.3 0.0 collective-permute-done.3
  26.4 0.0 copy-start
  26.4 1.4 copy-done
  27.8 0.0 copy-done.3
  27.8 95.4 %while.15 = (s32[]{:T(128)}, f32[960,640]{1,0:T(8,128)S(1)}, f32[4,640]{1,0:T(4,128)S(1)}, f32[4]{0:T(128)S(1)}, f32[4,960]{1,0:T(4,128)}, /*index=5*/f32[960,64...) while((s32[]{:T(128)}, f32[960,640]{1,0:T(8,128)S(1)}, ...), condition=%wide.region_5.6_spmd.clone.clone.clone, body=%wide.region_2.5_spmd.clone.clone.clone.sunk | while | flops 9280963 | bytes 7459999 | solution.py:64
  27.8 0.6 dynamic_slice.32
  28.5 0.7 constant_dynamic-slice_fusion.2
  29.2 0.1 multiply_reduce_fusion.7
  29.3 0.1 fusion.43
  29.5 0.7 add_add_fusion.4
  30.2 11.8 %fusion.44 = (f32[960]{0:T(1024)S(1)}, f32[960]{0:T(1024)S(1)}) fusion(f32[960,640]{1,0:T(8,128)} %get-tuple-element.333, f32[640]{0:T(1024)S(1)} %add_add_fusion.4, f32[960]{0:T(1024)S(1)} %add_multiply_fusion.2, f32[640]{0:T(1024)S(1)} %get-tuple-element.303), kind=kLoop, calls=%fused_computation.9.clone.1 | loop fusion | flops 4298880 | bytes 2474240 | tf_op jit(solution)/shard_map/while/body/eval_jaxpr/reduce_sum | solution.py:55
  42.0 9.7 %fusion.46 = f32[960,640]{1,0:T(8,128)S(1)} fusion(f32[960,640]{1,0:T(8,128)S(1)} %get-tuple-element.319, f32[960]{0:T(1024)S(1)} %get-tuple-element.306, f32[960]{0:T(1024)S(1)} %get-tuple-element.307, f32[640]{0:T(1024)S(1)} %add_add_fusion.4, f32[960]{0:T(1024)S(1)} %add_multiply_fusion.2, f32[640]{0:T(1024)S(1)} %get-tuple-element.303, ...), kind=kLoop, calls=%fused_computation.11.clone.1 | loop fusion | flops 4915200 | bytes 4931841 | tf_op jit(solution)/shard_map/while/body/eval_jaxpr/add | solution.py:58
  51.7 0.7 dynamic_slice.32
  52.3 0.7 constant_dynamic-slice_fusion.2
  53.1 0.1 multiply_reduce_fusion.7
  53.2 0.1 fusion.43
  53.3 0.7 add_add_fusion.4
  54.0 11.8 %fusion.44 = (f32[960]{0:T(1024)S(1)}, f32[960]{0:T(1024)S(1)}) fusion(f32[960,640]{1,0:T(8,128)} %get-tuple-element.333, f32[640]{0:T(1024)S(1)} %add_add_fusion.4, f32[960]{0:T(1024)S(1)} %add_multiply_fusion.2, f32[640]{0:T(1024)S(1)} %get-tuple-element.303), kind=kLoop, calls=%fused_computation.9.clone.1 | loop fusion | flops 4298880 | bytes 2474240 | tf_op jit(solution)/shard_map/while/body/eval_jaxpr/reduce_sum | solution.py:55
  65.8 9.7 %fusion.46 = f32[960,640]{1,0:T(8,128)S(1)} fusion(f32[960,640]{1,0:T(8,128)S(1)} %get-tuple-element.319, f32[960]{0:T(1024)S(1)} %get-tuple-element.306, f32[960]{0:T(1024)S(1)} %get-tuple-element.307, f32[640]{0:T(1024)S(1)} %add_add_fusion.4, f32[960]{0:T(1024)S(1)} %add_multiply_fusion.2, f32[640]{0:T(1024)S(1)} %get-tuple-element.303, ...), kind=kLoop, calls=%fused_computation.11.clone.1 | loop fusion | flops 4915200 | bytes 4931841 | tf_op jit(solution)/shard_map/while/body/eval_jaxpr/add | solution.py:58
  75.5 0.7 dynamic_slice.32
  76.2 0.7 constant_dynamic-slice_fusion.2
  76.9 0.1 multiply_reduce_fusion.7
  77.0 0.1 fusion.43
  77.2 0.7 add_add_fusion.4
  77.8 11.8 %fusion.44 = (f32[960]{0:T(1024)S(1)}, f32[960]{0:T(1024)S(1)}) fusion(f32[960,640]{1,0:T(8,128)} %get-tuple-element.333, f32[640]{0:T(1024)S(1)} %add_add_fusion.4, f32[960]{0:T(1024)S(1)} %add_multiply_fusion.2, f32[640]{0:T(1024)S(1)} %get-tuple-element.303), kind=kLoop, calls=%fused_computation.9.clone.1 | loop fusion | flops 4298880 | bytes 2474240 | tf_op jit(solution)/shard_map/while/body/eval_jaxpr/reduce_sum | solution.py:55
  89.7 9.7 %fusion.46 = f32[960,640]{1,0:T(8,128)S(1)} fusion(f32[960,640]{1,0:T(8,128)S(1)} %get-tuple-element.319, f32[960]{0:T(1024)S(1)} %get-tuple-element.306, f32[960]{0:T(1024)S(1)} %get-tuple-element.307, f32[640]{0:T(1024)S(1)} %add_add_fusion.4, f32[960]{0:T(1024)S(1)} %add_multiply_fusion.2, f32[640]{0:T(1024)S(1)} %get-tuple-element.303, ...), kind=kLoop, calls=%fused_computation.11.clone.1 | loop fusion | flops 4915200 | bytes 4931841 | tf_op jit(solution)/shard_map/while/body/eval_jaxpr/add | solution.py:58
  99.4 0.7 dynamic_slice.32
  100.0 0.7 constant_dynamic-slice_fusion.2
  100.7 0.1 multiply_reduce_fusion.7
  100.9 0.1 fusion.43
  101.0 0.7 add_add_fusion.4
  101.7 11.8 %fusion.44 = (f32[960]{0:T(1024)S(1)}, f32[960]{0:T(1024)S(1)}) fusion(f32[960,640]{1,0:T(8,128)} %get-tuple-element.333, f32[640]{0:T(1024)S(1)} %add_add_fusion.4, f32[960]{0:T(1024)S(1)} %add_multiply_fusion.2, f32[640]{0:T(1024)S(1)} %get-tuple-element.303), kind=kLoop, calls=%fused_computation.9.clone.1 | loop fusion | flops 4298880 | bytes 2474240 | tf_op jit(solution)/shard_map/while/body/eval_jaxpr/reduce_sum | solution.py:55
  113.5 9.7 %fusion.46 = f32[960,640]{1,0:T(8,128)S(1)} fusion(f32[960,640]{1,0:T(8,128)S(1)} %get-tuple-element.319, f32[960]{0:T(1024)S(1)} %get-tuple-element.306, f32[960]{0:T(1024)S(1)} %get-tuple-element.307, f32[640]{0:T(1024)S(1)} %add_add_fusion.4, f32[960]{0:T(1024)S(1)} %add_multiply_fusion.2, f32[640]{0:T(1024)S(1)} %get-tuple-element.303, ...), kind=kLoop, calls=%fused_computation.11.clone.1 | loop fusion | flops 4915200 | bytes 4931841 | tf_op jit(solution)/shard_map/while/body/eval_jaxpr/add | solution.py:58
  123.2 0.0 copy-start.1
  123.2 0.0 copy-start.2
  123.2 0.1 fusion.38
  123.3 4.5 %collective-permute-start.4 = (f32[960,128]{1,0:T(8,128)S(1)}, f32[960,128]{1,0:T(8,128)S(1)}, u32[]{:S(2)}, u32[]{:S(2)}) collective-permute-start(f32[960,128]{1,0:T(8,128)S(1)} %get-tuple-element.240), channel_id=1, source_target_pairs={{0,2},{2,4},{4,6},{6,8},{8,10},{10,12},{12,14},{14,16},{16,18},{18... | collective-permute-start | bytes 1474568 | tf_op jit(solution)/shard_map/ppermute | solution.py:23
  127.8 0.0 collective-permute-start.6
  127.8 6.6 %collective-permute-done.4 = f32[960,128]{1,0:T(8,128)S(1)} collective-permute-done((f32[960,128]{1,0:T(8,128)S(1)}, f32[960,128]{1,0:T(8,128)S(1)}, u32[]{:S(2)}, u32[]{:S(2)}) %collective-permute-start.4) | collective-permute-done | bytes 491552 | tf_op jit(solution)/shard_map/ppermute | solution.py:23
  134.4 0.0 collective-permute-done.6
  134.4 0.1 slice_add_fusion.1
  134.5 6.2 %collective-permute-start.5 = (f32[960,128]{1,0:T(8,128)S(1)}, f32[960,128]{1,0:T(8,128)S(1)}, u32[]{:S(2)}, u32[]{:S(2)}) collective-permute-start(f32[960,128]{1,0:T(8,128)S(1)} %get-tuple-element.238), channel_id=1, source_target_pairs={{0,2},{2,4},{4,6},{6,8},{8,10},{10,12},{12,14},{14,16},{16,18},{18... | collective-permute-start | bytes 1474568 | tf_op jit(solution)/shard_map/ppermute | solution.py:23
  140.7 0.0 collective-permute-start.7
  140.7 4.8 %collective-permute-done.5 = f32[960,128]{1,0:T(8,128)S(1)} collective-permute-done((f32[960,128]{1,0:T(8,128)S(1)}, f32[960,128]{1,0:T(8,128)S(1)}, u32[]{:S(2)}, u32[]{:S(2)}) %collective-permute-start.5) | collective-permute-done | bytes 491552 | tf_op jit(solution)/shard_map/ppermute | solution.py:23
  145.5 1.5 collective-permute-done.7
  147.0 0.0 copy-done.1
  147.0 0.0 copy-done.2
  147.0 1.6 multiply_reduce_fusion.2
  148.7 49.7 %all-reduce = (f32[]{:T(128)}, f32[]{:T(128)}, f32[]{:T(128)}, f32[]{:T(128)}) all-reduce(f32[]{:T(128)} %get-tuple-element.207, f32[]{:T(128)} %get-tuple-element.208, f32[]{:T(128)} %get-tuple-element.206, f32[]{:T(128)} %get-tuple-element.205), channel_id=1, replica_groups=mesh['ra'=16,'freq'=2] {'ra','freq'}, use_global_device_ids=true, to_apply=%region_1.2 | all-reduce | flops 4 | bytes 32 | tf_op jit(solution)/shard_map/psum | solution.py:112
  201.7 2.4 %multiply_add_fusion = (f32[960,128]{1,0:T(8,128)}, f32[960,128]{1,0:T(8,128)}, f32[960,128]{1,0:T(8,128)}) fusion(f32[960,128]{1,0:T(8,128)S(1)} %copy-done.1, f32[]{:T(128)S(6)} %div.39, f32[960,128]{1,0:T(8,128)S(1)} %copy-done.2, f32[960,128]{1,0:T(8,128)} %get-tuple-element.231, f32[]{:T(128)S(6)} %div.38, f32[960,128]{1,0:T(8,128)} %param.9), kind=kLoop, calls=%fused_computation.56 | loop fusion | flops 737280 | bytes 3440648 | tf_op jit(solution)/shard_map/add | solution.py:126
  (12 shorter events, 0.2 us)
Async XLA Ops:
  0.6 12.3 %collective-permute-start = (f32[960,128]{1,0:T(8,128)}, f32[960,128]{1,0:T(8,128)S(1)}, u32[]{:S(2)}, u32[]{:S(2)}) collective-permute-start(f32[960,128]{1,0:T(8,128)} %param.11), channel_id=1, source_target_pairs={{0,2},{2,4},{4,6},{6,8},{8,10},{10,12},{12,14},{14,16},{16,18},{18... | collective-permute-start | bytes 1474568 | tf_op jit(solution)/shard_map/ppermute | solution.py:23
  1.2 15.5 %collective-permute-start.2 = (f32[960,128]{1,0:T(8,128)}, f32[960,128]{1,0:T(8,128)S(1)}, u32[]{:S(2)}, u32[]{:S(2)}) collective-permute-start(f32[960,128]{1,0:T(8,128)} %param.11), channel_id=1, source_target_pairs={{0,30},{2,0},{4,2},{6,4},{8,6},{10,8},{12,10},{14,12},{16,14},{18,... | collective-permute-start | bytes 1474568 | tf_op jit(solution)/shard_map/ppermute | solution.py:23
  13.0 11.2 %collective-permute-start.1 = (f32[960,128]{1,0:T(8,128)S(1)}, f32[960,128]{1,0:T(8,128)}, u32[]{:S(2)}, u32[]{:S(2)}) collective-permute-start(f32[960,128]{1,0:T(8,128)S(1)} %collective-permute-done), channel_id=1, source_target_pairs={{0,2},{2,4},{4,6},{6,8},{8,10},{10,12},{12,14},{14,16},{16,18},{18... | collective-permute-start | bytes 1474568 | tf_op jit(solution)/shard_map/ppermute | solution.py:23
  16.7 11.2 %copy-start.3 = (f32[4]{0:T(128)S(1)}, f32[4]{0:T(128)}, u32[]{:S(2)}) copy-start(f32[4]{0:T(128)} %param.12) | copy-start | bytes 52
  16.7 9.7 %collective-permute-start.3 = (f32[960,128]{1,0:T(8,128)S(1)}, f32[960,128]{1,0:T(8,128)S(1)}, u32[]{:S(2)}, u32[]{:S(2)}) collective-permute-start(f32[960,128]{1,0:T(8,128)S(1)} %collective-permute-done.2), channel_id=1, source_target_pairs={{0,30},{2,0},{4,2},{6,4},{8,6},{10,8},{12,10},{14,12},{16,14},{18,... | collective-permute-start | bytes 1474568 | tf_op jit(solution)/shard_map/ppermute | solution.py:23
  26.4 1.4 copy-start
  123.2 23.8 %copy-start.1 = (f32[960,128]{1,0:T(8,128)S(1)}, f32[960,128]{1,0:T(8,128)}, u32[]{:S(2)}) copy-start(f32[960,128]{1,0:T(8,128)} %param.11) | copy-start | bytes 1474564
  123.2 23.8 %copy-start.2 = (f32[960,128]{1,0:T(8,128)S(1)}, f32[960,128]{1,0:T(8,128)}, u32[]{:S(2)}) copy-start(f32[960,128]{1,0:T(8,128)} %param.10) | copy-start | bytes 1474564
  123.3 11.1 %collective-permute-start.4 = (f32[960,128]{1,0:T(8,128)S(1)}, f32[960,128]{1,0:T(8,128)S(1)}, u32[]{:S(2)}, u32[]{:S(2)}) collective-permute-start(f32[960,128]{1,0:T(8,128)S(1)} %get-tuple-element.240), channel_id=1, source_target_pairs={{0,2},{2,4},{4,6},{6,8},{8,10},{10,12},{12,14},{14,16},{16,18},{18... | collective-permute-start | bytes 1474568 | tf_op jit(solution)/shard_map/ppermute | solution.py:23
  127.8 6.6 %collective-permute-start.6 = (f32[960,128]{1,0:T(8,128)S(1)}, f32[960,128]{1,0:T(8,128)S(1)}, u32[]{:S(2)}, u32[]{:S(2)}) collective-permute-start(f32[960,128]{1,0:T(8,128)S(1)} %get-tuple-element.241), channel_id=1, source_target_pairs={{0,30},{2,0},{4,2},{6,4},{8,6},{10,8},{12,10},{14,12},{16,14},{18,... | collective-permute-start | bytes 1474568 | tf_op jit(solution)/shard_map/ppermute | solution.py:23
  134.5 11.0 %collective-permute-start.5 = (f32[960,128]{1,0:T(8,128)S(1)}, f32[960,128]{1,0:T(8,128)S(1)}, u32[]{:S(2)}, u32[]{:S(2)}) collective-permute-start(f32[960,128]{1,0:T(8,128)S(1)} %get-tuple-element.238), channel_id=1, source_target_pairs={{0,2},{2,4},{4,6},{6,8},{8,10},{10,12},{12,14},{14,16},{16,18},{18... | collective-permute-start | bytes 1474568 | tf_op jit(solution)/shard_map/ppermute | solution.py:23
  140.7 6.4 %collective-permute-start.7 = (f32[960,128]{1,0:T(8,128)S(1)}, f32[960,128]{1,0:T(8,128)S(1)}, u32[]{:S(2)}, u32[]{:S(2)}) collective-permute-start(f32[960,128]{1,0:T(8,128)S(1)} %get-tuple-element.239), channel_id=1, source_target_pairs={{0,30},{2,0},{4,2},{6,4},{8,6},{10,8},{12,10},{14,12},{16,14},{18,... | collective-permute-start | bytes 1474568 | tf_op jit(solution)/shard_map/ppermute | solution.py:23
where the time goes:
time: 205 us; the launch traced here: 204 us
  other arithmetic  95.2 us (46%)
  blocking collectives  49.7 us (24%)
  waiting for transfers between devices  24.8 us (12%)
  starting transfers between devices  20.7 us (10%)
  local copies, waits for them, and re-layouts  9.39 us (5%)
  between operations  4.01 us (2%)
    psum x1, blocking collectives, shards(): lax.psum((jnp.sum(residual * residual), jnp.sum(direction * image), jnp.s...  49.7 us
    reduce_sum x4, other arithmetic, one_segment(): fwd_real = jnp.sum(cos_tile * window, axis=1)  47.3 us
    add x4, other arithmetic, one_segment(): running + cos_tile * (noise_row * fwd_real)[:, None]  38.7 us
    ppermute x8, waiting for transfers between devices, from_behind(): return lax.ppermute(value, axis, pairs)  24.8 us
    ppermute x8, starting transfers between devices, from_behind(): return lax.ppermute(value, axis, pairs)  20.7 us
    dynamic_slice x8, local copies, waits for them, and re-layouts, segment_images(): lax.scan(one_segment, jnp.zeros(window.shape, jnp.float32), (sid_angles,...  5.49 us
  transfers between devices with their start and end apart: 8, of which 5 were waited for; matrix products, arithmetic and copies ran while one was open for 2% of the time, Pallas kernels for 0%

commit v1 on v0

v1 whole, which is shorter than its diff:
```python
import functools
import math

import jax
import jax.numpy as jnp
import numpy as np
from jax import lax
from jax.experimental import pallas as pl
from jax.experimental.pallas import tpu as pltpu
from jax.sharding import PartitionSpec as P

NDEC = 64
RA_DEV = 2
SPAN = 256

TWO_PI = 6.283185307179586
baseline_x = -0.006
baseline_y = 0.007
baseline_z = 0.0035
low_freq = 20.0
bin_width = 0.25
epsilon = 1e-06
MESH = pl.DeviceIdType.MESH
OFFSETS = (-2, -1, 1, 2)


def poly_fit(function, high, degree):
    fit = np.polynomial.chebyshev.Chebyshev.interpolate(function, degree, domain=[0.0, high])
    return [float(c) for c in fit.convert(kind=np.polynomial.Polynomial).coef]


def sinc_turns(z):
    r = np.sqrt(z)
    return 2 * np.pi * np.sinc(2 * r)


COS_COEF = poly_fit(lambda z: np.cos(2 * np.pi * np.sqrt(z)), 0.25, 9)
SIN_COEF = poly_fit(sinc_turns, 0.25, 8)


def horner(coef, z):
    total = jnp.full_like(z, coef[-1])
    for c in coef[-2::-1]:
        total = total * z + c
    return total


def reduce_turns(p):
    return p - jnp.floor(p + 0.5)


def cos_turns(p):
    r = reduce_turns(p)
    return horner(COS_COEF, r * r)


def sincos_turns(p):
    r = reduce_turns(p)
    z = r * r
    return r * horner(SIN_COEF, z), horner(COS_COEF, z)


def node_count():
    reach = math.sqrt(baseline_x**2 + baseline_y**2 + baseline_z**2)
    c = math.pi * bin_width * SPAN * reach
    count = 2
    while 2 * (c / 2) ** count / math.factorial(count) > 3e-8:
        count += 2
    return count


def lagrange_rows(count):
    half = (SPAN - 1) / 2
    nodes = np.cos(np.pi * (2 * np.arange(count) + 1) / (2 * count))
    x = (np.arange(SPAN) - half) / half
    rows = []
    for r in range(count):
        row = np.ones(SPAN)
        for j in range(count):
            if j != r:
                row = row * (x - nodes[j]) / (nodes[r] - nodes[j])
        rows.append(row)
    return nodes, np.stack(rows).astype(np.float32)


def split(x):
    high = x.astype(jnp.bfloat16)
    return high, (x - high.astype(jnp.float32)).astype(jnp.bfloat16)


def kernel(
    n, m, nodes,
    sid_ref, resp_ref, sig_ref, noise_ref, lag_ref, dir_ref, res_ref,
    img_ref, ab_ref,
    asend, abuf, fsend, fbuf, gsend, gbuf, vh_ref, vl_ref, dsend, dbuf, esend, ebuf,
    a_ss, a_rs, b_ss, b_rs, c_ss, c_rs, d_ss, d_rs, e_ss, e_rs,
):
    me = lax.axis_index("ra")
    band = lax.axis_index("freq")
    count = len(nodes)
    seg = resp_ref.shape[0]
    pix = dir_ref.shape[1]
    bins = dir_ref.shape[0]
    chunks = [(k, min(k + SPAN, bins)) for k in range(0, bins, SPAN)]

    def ra_of(d):
        return lax.rem(me + d + n, n)

    barrier = pltpu.get_barrier_semaphore()
    for d in range(1, n):
        pl.semaphore_signal(barrier, inc=1, device_id={"ra": ra_of(d)}, device_id_type=MESH)
    for d in range(1, m):
        pl.semaphore_signal(
            barrier, inc=1, device_id={"freq": lax.rem(band + d, m)}, device_id_type=MESH
        )

    lane = lax.broadcasted_iota(jnp.int32, (seg, pix), 1)
    for g in range(5):
        kept = jnp.zeros((seg, pix), jnp.float32)
        for j in range(RA_DEV):
            col = jnp.broadcast_to(
                sig_ref[:, g * RA_DEV + j : g * RA_DEV + j + 1].astype(jnp.float32), (seg, pix)
            )
            kept = jnp.where(lane // NDEC == j, col, kept)
        w = resp_ref[:, g * pix : (g + 1) * pix] * kept
        asend[g, 0:seg, :] = w
        asend[g, seg : 2 * seg, :] = w
        for s in range(2 * seg):
            asend[g, 2 * seg + s : 2 * seg + s + 1, :] = jnp.full((1, pix), sid_ref[s % seg])
    abuf[2] = asend[2]
    dh, dl = split(dir_ref[...])
    dcat = jnp.concatenate([dh, dh, dl], axis=1)
    residual = res_ref[...]
    rr = jnp.sum(residual * residual, axis=0, keepdims=True)

    pl.semaphore_wait(barrier, n - 1 + m - 1)

    def remote(src, dst, ss, rs, where):
        return pltpu.make_async_remote_copy(
            src_ref=src, dst_ref=dst, send_sem=ss, recv_sem=rs, device_id=where, device_id_type=MESH
        )

    a_copies = []
    for d in OFFSETS:
        g = d + 2
        cp = remote(asend.at[g], abuf.at[g], a_ss.at[g], a_rs.at[g], {"ra": ra_of(d)})
        cp.start()
        a_copies.append(cp)

    lane1 = lax.broadcasted_iota(jnp.int32, (1, pix), 1)
    column = (me * RA_DEV + lane1 // NDEC).astype(jnp.float32)
    dec_row = (lane1 % NDEC).astype(jnp.float32)
    ra_turns = (column + 0.5) / (RA_DEV * n)
    sin_dec, cos_dec = sincos_turns(0.5 * ((dec_row + 0.5) / NDEC - 0.5))

    for cp in a_copies:
        cp.wait()

    rows = 10 * seg
    weight = jnp.concatenate([abuf[g, 0 : 2 * seg, :] for g in range(5)], axis=0)
    sid = jnp.concatenate([abuf[g, 2 * seg : 4 * seg, :] for g in range(5)], axis=0)
    sin_h, cos_h = sincos_turns(ra_turns - sid * (1.0 / TWO_PI))
    delay = cos_dec * (baseline_x * cos_h + baseline_y * sin_h) + baseline_z * sin_dec
    row_id = lax.broadcasted_iota(jnp.int32, (rows, pix), 0)
    shift = jnp.where(lax.rem(row_id, 2 * seg) >= seg, 0.25, 0.0)
    half = bin_width * (SPAN - 1) / 2
    fine = [sincos_turns((half * float(nodes[r])) * delay) for r in range(count // 2)]

    for index, (k0, k1) in enumerate(chunks):
        centre = low_freq + bin_width * (
            (band * bins + k0).astype(jnp.float32) + (SPAN - 1) / 2
        )
        p = reduce_turns(centre * delay)
        t0 = weight * cos_turns(p - shift)
        t1 = weight * cos_turns(p - shift + 0.25)
        up, down = [], []
        for sin_d, cos_d in fine:
            a, b = t0 * cos_d, t1 * sin_d
            up.append(a + b)
            down.append(a - b)
        table = jnp.concatenate(up + down[::-1], axis=0)
        vh, vl = split(table)
        vh_ref[index] = vh
        vl_ref[index] = vl
        product = lax.dot_general(
            jnp.concatenate([vh, vl, vh], axis=1), dcat[k0:k1],
            (((1,), (1,)), ((), ())), preferred_element_type=jnp.float32,
        )
        total = lag_ref[0:1, 0 : k1 - k0] * product[0:rows]
        for r in range(1, count):
            total = total + lag_ref[r : r + 1, 0 : k1 - k0] * product[r * rows : (r + 1) * rows]
        for g in range(5):
            fsend[g, :, k0:k1] = total[g * 2 * seg : (g + 1) * 2 * seg]

    b_copies = []
    for d in OFFSETS:
        g = d + 2
        cp = remote(fsend.at[g], fbuf.at[g], b_ss.at[g], b_rs.at[g], {"ra": ra_of(-d)})
        cp.start()
        b_copies.append(cp)
    noise = jnp.concatenate([noise_ref[...], noise_ref[...]], axis=0)
    for cp in b_copies:
        cp.wait()
    forward = fsend[2]
    for d in OFFSETS:
        forward = forward + fbuf[d + 2]
    weighted = noise * forward
    gsend[...] = weighted
    c_copies = []
    for d in OFFSETS:
        g = d + 2
        cp = remote(gsend, gbuf.at[g], c_ss.at[g], c_rs.at[g], {"ra": ra_of(d)})
        cp.start()
        c_copies.append(cp)
    gbuf[2] = weighted
    power = jnp.sum(weighted * forward)
    for cp in c_copies:
        cp.wait()

    cross = jnp.zeros((1, pix), jnp.float32)
    norm = jnp.zeros((1, pix), jnp.float32)
    for index, (k0, k1) in enumerate(chunks):
        g = jnp.concatenate([gbuf[j, :, k0:k1] for j in range(5)], axis=0)
        spread = jnp.concatenate(
            [lag_ref[r : r + 1, 0 : k1 - k0] * g for r in range(count)], axis=0
        )
        gh, gl = split(spread)
        vh, vl = vh_ref[index], vl_ref[index]
        image_t = lax.dot_general(
            jnp.concatenate([vh, vl, vh], axis=0), jnp.concatenate([gh, gh, gl], axis=0),
            (((0,), (0,)), ((), ())), preferred_element_type=jnp.float32,
        )
        image = image_t.T
        img_ref[k0:k1, :] = image
        cross = cross + jnp.sum(image * res_ref[k0:k1, :], axis=0, keepdims=True)
        norm = norm + jnp.sum(image * image, axis=0, keepdims=True)

    dsend[0:1, :] = rr
    dsend[1:2, :] = jnp.where(lane1 == 0, power, 0.0)
    dsend[2:3, :] = cross
    dsend[3:4, :] = norm
    dsend[4:8, :] = jnp.zeros((4, pix), jnp.float32)
    d_copies = []
    for d in range(1, m):
        cp = remote(
            dsend, dbuf.at[d], d_ss.at[d], d_rs.at[d], {"freq": lax.rem(band + d, m)}
        )
        cp.start()
        d_copies.append(cp)
    for cp in d_copies:
        cp.wait()
    sums = dsend[...]
    for d in range(1, m):
        sums = sums + dbuf[d]
    esend[...] = sums
    e_copies = []
    for d in range(1, n):
        cp = remote(esend, ebuf.at[d], e_ss.at[d], e_rs.at[d], {"ra": ra_of(d)})
        cp.start()
        e_copies.append(cp)
    for cp in e_copies:
        cp.wait()
    for d in range(1, n):
        sums = sums + ebuf[d]
    sums = jnp.sum(sums, axis=1, keepdims=True)
    rr_all, power_all, cross_all, norm_all = (sums[i : i + 1] for i in range(4))
    alpha = (rr_all + epsilon) / (power_all + epsilon)
    beta = (rr_all - 2.0 * alpha * cross_all + alpha * alpha * norm_all) / (rr_all + epsilon)
    ab_ref[0:1, :] = jnp.broadcast_to(alpha, (1, pix))
    ab_ref[1:2, :] = jnp.broadcast_to(beta, (1, pix))
    ab_ref[2:8, :] = jnp.zeros((6, pix), jnp.float32)


def solution(mesh):
    n, m = mesh.shape["ra"], mesh.shape["freq"]

    def shards(estimate, residual, direction, sidereal, response, significant, inv_noise):
        bins, pix = direction.shape
        seg = sidereal.shape[0]
        count = node_count()
        nodes, lagrange = lagrange_rows(count)
        pieces = -(-bins // SPAN)
        f32, bf16 = jnp.float32, jnp.bfloat16
        vmem = pl.BlockSpec(memory_space=pltpu.VMEM)
        dma = pltpu.SemaphoreType.DMA
        image, steps = pl.pallas_call(
            functools.partial(kernel, n, m, nodes),
            out_shape=(
                jax.ShapeDtypeStruct((bins, pix), f32),
                jax.ShapeDtypeStruct((8, pix), f32),
            ),
            in_specs=[pl.BlockSpec(memory_space=pltpu.SMEM)] + [vmem] * 6,
            out_specs=(vmem, vmem),
            scratch_shapes=[
                pltpu.VMEM((5, 4 * seg, pix), f32),
                pltpu.VMEM((5, 4 * seg, pix), f32),
                pltpu.VMEM((5, 2 * seg, bins), f32),
                pltpu.VMEM((5, 2 * seg, bins), f32),
                pltpu.VMEM((2 * seg, bins), f32),
                pltpu.VMEM((5, 2 * seg, bins), f32),
                pltpu.VMEM((pieces, count * 10 * seg, pix), bf16),
                pltpu.VMEM((pieces, count * 10 * seg, pix), bf16),
                pltpu.VMEM((8, pix), f32),
                pltpu.VMEM((m, 8, pix), f32),
                pltpu.VMEM((8, pix), f32),
                pltpu.VMEM((n, 8, pix), f32),
            ]
            + [dma((5,))] * 6
            + [dma((m,))] * 2
            + [dma((n,))] * 2,
            compiler_params=pltpu.CompilerParams(collective_id=0, has_side_effects=True),
        )(sidereal, response, significant, inv_noise, jnp.asarray(lagrange), direction, residual)
        alpha, beta = steps[0, 0], steps[1, 0]
        residual_next = residual - alpha * image
        return (
            estimate + alpha * direction,
            residual_next,
            residual_next + beta * direction,
        )

    return jax.shard_map(
        shards,
        mesh=mesh,
        in_specs=(
            P("freq", "ra"),
            P("freq", "ra"),
            P("freq", "ra"),
            P("ra"),
            P("ra", None),
            P("ra", None),
            P("ra", "freq"),
        ),
        out_specs=(P("freq", "ra"), P("freq", "ra"), P("freq", "ra")),
        check_vma=False,
    )
```

time: 205 us -> 36.1 us (0.18)
  other arithmetic: 95.2 us -> 3.59 us
  blocking collectives: 49.7 us -> 0 us
  Pallas kernels: 0 us -> 30.3 us
  waiting for transfers between devices: 24.8 us -> 0 us
  starting transfers between devices: 20.7 us -> 0 us
  local copies, waits for them, and re-layouts: 9.39 us -> 1.34 us
  between operations: 4.01 us -> 0.66 us
    psum x1 -> x0, blocking collectives: 49.7 us -> none  [shards(): lax.psum((jnp.sum(residual * residual), jnp.sum(direction * image), jnp.s...]
    reduce_sum x5 -> x0, other arithmetic: 48.9 us -> none  [the longest x4 47.3 us: one_segment(): fwd_real = jnp.sum(cos_tile * window, axis=1)]
    add x10 -> x1, other arithmetic: 43.9 us -> 3.59 us  [shards(): residual_next + beta * direction]
    pallas_call x0 -> x1, Pallas kernels: none -> 30.3 us  [shards(): pl.pallas_call(functools.partial(kernel, n, m, nodes), out_shape=(jax.Sha...]
    ppermute x8 -> x0, waiting for transfers between devices: 24.8 us -> none  [from_behind(): return lax.ppermute(value, axis, pairs)]
    ppermute x8 -> x0, starting transfers between devices: 20.7 us -> none  [from_behind(): return lax.ppermute(value, axis, pairs)]
    dynamic_slice x8 -> x0, local copies, waits for them, and re-layouts: 5.49 us -> none  [segment_images(): lax.scan(one_segment, jnp.zeros(window.shape, jnp.float32), (sid_angles,...]
    unnamed x12 -> x4, local copies, waits for them, and re-layouts: 3.65 us -> 0.01 us
  transfers between devices with their start and end apart: 8 -> 0, of which waited for: 5 -> 0; matrix products, arithmetic and copies ran while one was open for 2% -> 0% of each run, Pallas kernels for 0% -> 0%
where the time goes in v1:
time: 36.1 us; the launch traced here: 35.9 us
  Pallas kernels  30.3 us (84%)
  other arithmetic  3.59 us (10%)
  local copies, waits for them, and re-layouts  1.34 us (4%)
  between operations  0.66 us (2%)
    pallas_call x1, Pallas kernels, shards(): pl.pallas_call(functools.partial(kernel, n, m, nodes), out_shape=(jax.Sha...  30.3 us
    add x1, other arithmetic, shards(): residual_next + beta * direction  3.59 us
    slice x1, local copies, waits for them, and re-layouts, shards(): alpha, beta = (steps[0, 0], steps[1, 0])  1.33 us

profile of v1, /device:TPU:0, one launch (start us, length us, event | category | flops | bytes accessed | tf_op | source)
XLA Modules:
  0.0 35.9 jit_solution(2665906229156325869)
XLA Ops:
  0.6 0.0 copy-start
  0.6 0.0 copy-start.1
  0.7 30.3 %shard_map.103 = (f32[960,128]{1,0:T(8,128)}, f32[8,128]{1,0:T(8,128)}) custom-call(f32[4]{0:T(128)} %sid_ref.1, f32[4,640]{1,0:T(4,128)} %resp_ref.1, s32[4,10]{1,0:T(4,128)} %sig_ref.1, f32[4,960]{1,0:T(4,128)} %noise_ref.1, f32[12,256]{1,0:T(8,128)} %constant.2.clone.lag_ref, f32[960,128]{1,0:T(8,128)} %dir_ref.1, f32[960,128]{1,0:T(8,128)} %res_ref.1), custom_call_target="tpu_custom_call" | custom-call | tf_op jit(solution)/shard_map/pallas_call | solution.py:286
  30.9 1.3 %fusion = (f32[1,1]{1,0:T(1,128)}, f32[1,1]{1,0:T(1,128)}) fusion(f32[8,128]{1,0:T(8,128)} %get-tuple-element.5), kind=kLoop, calls=%fused_computation.3 | loop fusion | bytes 16 | tf_op jit(solution)/shard_map/slice | solution.py:313
  32.3 0.0 copy-done
  32.3 0.0 copy-done.1
  32.3 3.6 %multiply_add_fusion = (f32[960,128]{1,0:T(8,128)}, f32[960,128]{1,0:T(8,128)}, f32[960,128]{1,0:T(8,128)}) fusion(f32[960,128]{1,0:T(8,128)S(1)} %copy-done, f32[]{:T(128)} %bitcast.1, f32[960,128]{1,0:T(8,128)S(1)} %copy-done.1, f32[960,128]{1,0:T(8,128)} %get-tuple-element.6, f32[]{:T(128)} %bitcast, f32[960,128]{1,0:T(8,128)} %param.8), kind=kLoop, calls=%fused_computation | loop fusion | flops 737280 | bytes 3440648 | tf_op jit(solution)/shard_map/add | solution.py:318
Async XLA Ops:
  0.6 31.6 %copy-start = (f32[960,128]{1,0:T(8,128)S(1)}, f32[960,128]{1,0:T(8,128)}, u32[]{:S(2)}) copy-start(f32[960,128]{1,0:T(8,128)} %dir_ref.1) | copy-start | bytes 1474564
  0.6 31.6 %copy-start.1 = (f32[960,128]{1,0:T(8,128)S(1)}, f32[960,128]{1,0:T(8,128)}, u32[]{:S(2)}) copy-start(f32[960,128]{1,0:T(8,128)} %res_ref.1) | copy-start | bytes 1474564

commit v2 on v1

v2 whole, which is shorter than its diff:
```python
import functools
import math

import jax
import jax.numpy as jnp
import numpy as np
from jax import lax
from jax.experimental import pallas as pl
from jax.experimental.pallas import tpu as pltpu
from jax.sharding import PartitionSpec as P

NDEC = 64
RA_DEV = 2
SPAN = 256

TWO_PI = 6.283185307179586
baseline_x = -0.006
baseline_y = 0.007
baseline_z = 0.0035
low_freq = 20.0
bin_width = 0.25
epsilon = 1e-06
MESH = pl.DeviceIdType.MESH
OFFSETS = (-2, -1, 1, 2)
UNROLL = 64


def poly_fit(function, high, degree):
    fit = np.polynomial.chebyshev.Chebyshev.interpolate(function, degree, domain=[0.0, high])
    return [float(c) for c in fit.convert(kind=np.polynomial.Polynomial).coef]


def sinc_turns(z):
    r = np.sqrt(z)
    return 2 * np.pi * np.sinc(2 * r)


COS_COEF = poly_fit(lambda z: np.cos(2 * np.pi * np.sqrt(z)), 0.25, 9)
SIN_COEF = poly_fit(sinc_turns, 0.25, 8)


def horner(coef, z):
    total = jnp.full_like(z, coef[-1])
    for c in coef[-2::-1]:
        total = total * z + c
    return total


def reduce_turns(p):
    return p - jnp.floor(p + 0.5)


def cos_turns(p):
    r = reduce_turns(p)
    return horner(COS_COEF, r * r)


def sincos_turns(p):
    r = reduce_turns(p)
    z = r * r
    return r * horner(SIN_COEF, z), horner(COS_COEF, z)


def node_count():
    reach = math.sqrt(baseline_x**2 + baseline_y**2 + baseline_z**2)
    c = math.pi * bin_width * SPAN * reach
    count = 2
    while 2 * (c / 2) ** count / math.factorial(count) > 3e-8:
        count += 2
    return count


def lagrange_rows(count):
    half = (SPAN - 1) / 2
    nodes = np.cos(np.pi * (2 * np.arange(count) + 1) / (2 * count))
    x = (np.arange(SPAN) - half) / half
    rows = []
    for r in range(count):
        row = np.ones(SPAN)
        for j in range(count):
            if j != r:
                row = row * (x - nodes[j]) / (nodes[r] - nodes[j])
        rows.append(row)
    return nodes, np.stack(rows).astype(np.float32)


def split(x):
    high = x.astype(jnp.bfloat16)
    return high, (x - high.astype(jnp.float32)).astype(jnp.bfloat16)


def kernel(
    n, m, nodes,
    sid_hbm, resp_hbm, sig_hbm, noise_hbm, lag_hbm, dir_hbm, res_hbm, est_hbm,
    sol_out, res_out, dir_out,
    sid_ref, resp_ref, sig_ref, noise_ref, lag_ref, dir_ref, res_ref, est_ref,
    asend, abuf, fsend, fbuf, gsend, gbuf, vh_ref, vl_ref, psend, pbuf, esend, ebuf,
    in_s, a_ss, a_rs, b_ss, b_rs, c_ss, c_rs, p_ss, p_rs, e_ss, e_rs,
):
    me = lax.axis_index("ra")
    band = lax.axis_index("freq")
    count = len(nodes)
    seg = resp_ref.shape[0]
    pix = dir_ref.shape[1]
    bins = dir_ref.shape[0]
    chunks = [(k, min(k + SPAN, bins)) for k in range(0, bins, SPAN)]
    everyone = n * m

    def ra_of(d):
        return lax.rem(me + d + n, n)

    def peer(i):
        return {"ra": lax.rem(me + i // m, n), "freq": lax.rem(band + i % m, m)}

    def each_peer(action):
        if everyone <= UNROLL:
            for i in range(1, everyone):
                action(i)
        else:
            @pl.loop(1, everyone)
            def _(i):
                action(i)

    barrier = pltpu.get_barrier_semaphore()
    each_peer(
        lambda i: pl.semaphore_signal(barrier, inc=1, device_id=peer(i), device_id_type=MESH)
    )
    pairs = [
        (resp_hbm, resp_ref), (sig_hbm, sig_ref), (sid_hbm, sid_ref), (dir_hbm, dir_ref),
        (lag_hbm, lag_ref), (res_hbm, res_ref), (noise_hbm, noise_ref), (est_hbm, est_ref),
    ]
    loads = [pltpu.make_async_copy(a, b, in_s.at[j]) for j, (a, b) in enumerate(pairs)]
    for cp in loads:
        cp.start()
    tail = chunks[-1][1] - chunks[-1][0]
    if tail < SPAN:
        fsend[len(chunks) - 1] = jnp.zeros(fsend.shape[1:], jnp.float32)
        gsend[len(chunks) - 1] = jnp.zeros(gsend.shape[1:], jnp.float32)

    lane1 = lax.broadcasted_iota(jnp.int32, (1, pix), 1)
    column = (me * RA_DEV + lane1 // NDEC).astype(jnp.float32)
    dec_row = (lane1 % NDEC).astype(jnp.float32)
    ra_turns = (column + 0.5) / (RA_DEV * n)
    sin_dec, cos_dec = sincos_turns(0.5 * ((dec_row + 0.5) / NDEC - 0.5))

    for cp in loads[:3]:
        cp.wait()
    lane = lax.broadcasted_iota(jnp.int32, (seg, pix), 1)
    for g in range(5):
        kept = jnp.zeros((seg, pix), jnp.float32)
        for j in range(RA_DEV):
            col = jnp.broadcast_to(
                sig_ref[:, g * RA_DEV + j : g * RA_DEV + j + 1].astype(jnp.float32), (seg, pix)
            )
            kept = jnp.where(lane // NDEC == j, col, kept)
        w = resp_ref[:, g * pix : (g + 1) * pix] * kept
        asend[g, 0:seg, :] = w
        asend[g, seg : 2 * seg, :] = w
        for s in range(2 * seg):
            asend[g, 2 * seg + s : 2 * seg + s + 1, :] = jnp.full((1, pix), sid_ref[s % seg])
    abuf[2] = asend[2]
    for cp in loads[3:6]:
        cp.wait()
    dh, dl = split(dir_ref[...])
    dcat = jnp.concatenate([dh, dh, dl], axis=1)
    residual = res_ref[...]
    rr = jnp.sum(residual * residual, axis=0, keepdims=True)

    pl.semaphore_wait(barrier, everyone - 1)

    def remote(src, dst, ss, rs, where):
        return pltpu.make_async_remote_copy(
            src_ref=src, dst_ref=dst, send_sem=ss, recv_sem=rs, device_id=where, device_id_type=MESH
        )

    a_copies = []
    for d in OFFSETS:
        g = d + 2
        cp = remote(asend.at[g], abuf.at[g], a_ss.at[g], a_rs.at[g], {"ra": ra_of(d)})
        cp.start()
        a_copies.append(cp)
    for cp in loads[6:]:
        cp.wait()
    noise = jnp.concatenate([noise_ref[...], noise_ref[...]], axis=0)
    for cp in a_copies:
        cp.wait_recv()

    rows = 10 * seg
    weight = jnp.concatenate([abuf[g, 0 : 2 * seg, :] for g in range(5)], axis=0)
    sid = jnp.concatenate([abuf[g, 2 * seg : 4 * seg, :] for g in range(5)], axis=0)
    sin_h, cos_h = sincos_turns(ra_turns - sid * (1.0 / TWO_PI))
    delay = cos_dec * (baseline_x * cos_h + baseline_y * sin_h) + baseline_z * sin_dec
    row_id = lax.broadcasted_iota(jnp.int32, (rows, pix), 0)
    shift = jnp.where(lax.rem(row_id, 2 * seg) >= seg, 0.25, 0.0)
    half = bin_width * (SPAN - 1) / 2
    fine = [sincos_turns((half * float(nodes[r])) * delay) for r in range(count // 2)]

    b_copies = []
    for index, (k0, k1) in enumerate(chunks):
        centre = low_freq + bin_width * (
            (band * bins + k0).astype(jnp.float32) + (SPAN - 1) / 2
        )
        p = reduce_turns(centre * delay)
        t0 = weight * cos_turns(p - shift)
        t1 = weight * cos_turns(p - shift + 0.25)
        up, down = [], []
        for sin_d, cos_d in fine:
            a, b = t0 * cos_d, t1 * sin_d
            up.append(a + b)
            down.append(a - b)
        table = jnp.concatenate(up + down[::-1], axis=0)
        vh, vl = split(table)
        vh_ref[index] = vh
        vl_ref[index] = vl
        product = lax.dot_general(
            jnp.concatenate([vh, vl, vh], axis=1), dcat[k0:k1],
            (((1,), (1,)), ((), ())), preferred_element_type=jnp.float32,
        )
        total = lag_ref[0:1, 0 : k1 - k0] * product[0:rows]
        for r in range(1, count):
            total = total + lag_ref[r : r + 1, 0 : k1 - k0] * product[r * rows : (r + 1) * rows]
        for g in range(5):
            fsend[index, g, :, 0 : k1 - k0] = total[g * 2 * seg : (g + 1) * 2 * seg]
        for d in OFFSETS:
            g = d + 2
            cp = remote(
                fsend.at[index, g], fbuf.at[index, g],
                b_ss.at[index, g], b_rs.at[index, g], {"ra": ra_of(-d)},
            )
            cp.start()
            b_copies.append(cp)

    c_copies = []
    power = jnp.zeros((1, pix), jnp.float32)
    for index, (k0, k1) in enumerate(chunks):
        for cp in b_copies[index * 4 : index * 4 + 4]:
            cp.wait_recv()
        forward = fsend[index, 2, :, 0 : k1 - k0]
        for d in OFFSETS:
            forward = forward + fbuf[index, d + 2, :, 0 : k1 - k0]
        weighted = noise[:, k0:k1] * forward
        gsend[index, :, 0 : k1 - k0] = weighted
        for d in OFFSETS:
            g = d + 2
            cp = remote(
                gsend.at[index], gbuf.at[index, g],
                c_ss.at[index, g], c_rs.at[index, g], {"ra": ra_of(d)},
            )
            cp.start()
            c_copies.append(cp)
        gbuf[index, 2, :, 0 : k1 - k0] = weighted
        both = jnp.sum(weighted * forward, axis=0, keepdims=True)
        for q in range(0, k1 - k0, pix):
            piece = both[:, q : min(q + pix, k1 - k0)]
            if piece.shape[1] < pix:
                piece = jnp.concatenate(
                    [piece, jnp.zeros((1, pix - piece.shape[1]), jnp.float32)], axis=1
                )
            power = power + piece
    psend[0:1, 0:pix] = rr
    psend[0:1, pix : 2 * pix] = power

    def share(src, buf, ss, rs):
        each_peer(lambda i: remote(src, buf.at[i], ss.at[i], rs.at[i], peer(i)).start())

    def gathered(src, buf, ss, rs):
        each_peer(lambda i: remote(src, buf.at[i], ss.at[i], rs.at[i], peer(i)).wait_recv())
        return jnp.sum(buf[...], axis=0)

    def sent(src, buf, ss, rs):
        each_peer(lambda i: remote(src, buf.at[i], ss.at[i], rs.at[i], peer(i)).wait_send())

    pbuf[0] = psend[...]
    share(psend, pbuf, p_ss, p_rs)

    images = []
    for index, (k0, k1) in enumerate(chunks):
        for cp in c_copies[index * 4 : index * 4 + 4]:
            cp.wait_recv()
        g = jnp.concatenate([gbuf[index, j, :, 0 : k1 - k0] for j in range(5)], axis=0)
        spread = jnp.concatenate(
            [lag_ref[r : r + 1, 0 : k1 - k0] * g for r in range(count)], axis=0
        )
        gh, gl = split(spread)
        vh, vl = vh_ref[index], vl_ref[index]
        image_t = lax.dot_general(
            jnp.concatenate([vh, vl, vh], axis=0), jnp.concatenate([gh, gh, gl], axis=0),
            (((0,), (0,)), ((), ())), preferred_element_type=jnp.float32,
        )
        res_out[k0:k1, :] = image_t.T

    totals = gathered(psend, pbuf, p_ss, p_rs)
    rr_all = jnp.sum(totals[:, 0:pix], axis=1, keepdims=True) + epsilon
    alpha = rr_all / (jnp.sum(totals[:, pix : 2 * pix], axis=1, keepdims=True) + epsilon)
    residual_next = res_ref[...] - alpha * res_out[...]
    res_out[...] = residual_next
    norm = jnp.sum(residual_next * residual_next, axis=0, keepdims=True)
    esend[...] = norm
    ebuf[0] = norm
    share(esend, ebuf, e_ss, e_rs)
    sol_out[...] = est_ref[...] + alpha * dir_ref[...]
    for cp in a_copies + b_copies + c_copies:
        cp.wait_send()
    sent(psend, pbuf, p_ss, p_rs)
    norm_all = jnp.sum(gathered(esend, ebuf, e_ss, e_rs), axis=1, keepdims=True)
    beta = norm_all / rr_all
    dir_out[...] = res_out[...] + beta * dir_ref[...]
    sent(esend, ebuf, e_ss, e_rs)


def solution(mesh):
    n, m = mesh.shape["ra"], mesh.shape["freq"]

    def shards(estimate, residual, direction, sidereal, response, significant, inv_noise):
        bins, pix = direction.shape
        seg = sidereal.shape[0]
        count = node_count()
        nodes, lagrange = lagrange_rows(count)
        pieces = -(-bins // SPAN)
        f32, bf16 = jnp.float32, jnp.bfloat16
        vmem = pl.BlockSpec(memory_space=pltpu.VMEM)
        dma = pltpu.SemaphoreType.DMA
        operands = (
            sidereal, response, significant, inv_noise, jnp.asarray(lagrange),
            direction, residual, estimate,
        )
        return pl.pallas_call(
            functools.partial(kernel, n, m, nodes),
            out_shape=(jax.ShapeDtypeStruct((bins, pix), f32),) * 3,
            in_specs=[pl.BlockSpec(memory_space=pl.ANY)] * len(operands),
            out_specs=(vmem,) * 3,
            scratch_shapes=[pltpu.SMEM(sidereal.shape, f32)]
            + [pltpu.VMEM(x.shape, x.dtype) for x in operands[1:]]
            + [
                pltpu.VMEM((5, 4 * seg, pix), f32),
                pltpu.VMEM((5, 4 * seg, pix), f32),
                pltpu.VMEM((pieces, 5, 2 * seg, SPAN), f32),
                pltpu.VMEM((pieces, 5, 2 * seg, SPAN), f32),
                pltpu.VMEM((pieces, 2 * seg, SPAN), f32),
                pltpu.VMEM((pieces, 5, 2 * seg, SPAN), f32),
                pltpu.VMEM((pieces, count * 10 * seg, pix), bf16),
                pltpu.VMEM((pieces, count * 10 * seg, pix), bf16),
                pltpu.VMEM((1, 2 * pix), f32),
                pltpu.VMEM((n * m, 1, 2 * pix), f32),
                pltpu.VMEM((1, pix), f32),
                pltpu.VMEM((n * m, 1, pix), f32),
                dma((len(operands),)),
            ]
            + [dma((5,))] * 2
            + [dma((pieces, 5))] * 4
            + [dma((n * m,))] * 4,
            compiler_params=pltpu.CompilerParams(collective_id=0, has_side_effects=True),
        )(*operands)

    return jax.shard_map(
        shards,
        mesh=mesh,
        in_specs=(
            P("freq", "ra"),
            P("freq", "ra"),
            P("freq", "ra"),
            P("ra"),
            P("ra", None),
            P("ra", None),
            P("ra", "freq"),
        ),
        out_specs=(P("freq", "ra"), P("freq", "ra"), P("freq", "ra")),
        check_vma=False,
    )
```

time: 36.1 us -> 34.1 us (0.945)
  other arithmetic: 3.59 us -> 0 us
  local copies, waits for them, and re-layouts: 1.34 us -> 3.89 us
  Pallas kernels: 30.3 us -> 29.3 us
    unnamed x4 -> x7, local copies, waits for them, and re-layouts: 0.01 us -> 3.89 us
    add x1 -> x0, other arithmetic: 3.59 us -> none  [shards(): residual_next + beta * direction]
    slice x1 -> x0, local copies, waits for them, and re-layouts: 1.33 us -> none  [shards(): alpha, beta = (steps[0, 0], steps[1, 0])]
    pallas_call x1, Pallas kernels: 30.3 us -> 29.3 us  [shards(): pl.pallas_call(functools.partial(kernel, n, m, nodes), out_shape=(jax.Sha...]
where the time goes in v2:
time: 34.1 us; the launch traced here: 33.9 us
  Pallas kernels  29.3 us (86%)
  local copies, waits for them, and re-layouts  3.89 us (11%)
  between operations  0.65 us (2%)
    pallas_call x1, Pallas kernels, shards(): pl.pallas_call(functools.partial(kernel, n, m, nodes), out_shape=(jax.Sha...  29.3 us
    unnamed x7, local copies, waits for them, and re-layouts  3.89 us

profile of v2, /device:TPU:0, one launch (start us, length us, event | category | flops | bytes accessed | tf_op | source)
XLA Modules:
  0.0 33.9 jit_solution(2029866115280857609)
XLA Ops:
  0.6 29.3 %shard_map.103 = (f32[960,128]{1,0:T(8,128)}, f32[960,128]{1,0:T(8,128)}, f32[960,128]{1,0:T(8,128)}) custom-call(f32[4]{0:T(128)} %sid_hbm.1, f32[4,640]{1,0:T(4,128)} %resp_hbm.1, s32[4,10]{1,0:T(4,128)} %sig_hbm.1, f32[4,960]{1,0:T(4,128)} %noise_hbm.1, f32[12,256]{1,0:T(8,128)} %constant.2.clone.lag_hbm, f32[960,128]{1,0:T(8,128)} %dir_hbm.1, ...), custom_call_target="tpu_custom_call" | custom-call | tf_op jit(solution)/shard_map/pallas_call | solution.py:327
  30.0 0.0 copy-start.1
  30.0 1.9 %copy.14 = f32[960,128]{1,0:T(8,128)} copy(f32[960,128]{1,0:T(8,128)} %get-tuple-element.6) | data formatting | bytes 983040
  31.9 0.0 copy-done.1
  31.9 0.0 copy-start
  31.9 0.8 %copy.15 = f32[960,128]{1,0:T(8,128)} copy(f32[960,128]{1,0:T(8,128)S(1)} %copy-done.1) | data formatting | bytes 983040
  32.7 0.4 %copy-done = f32[960,128]{1,0:T(8,128)S(1)} copy-done((f32[960,128]{1,0:T(8,128)S(1)}, f32[960,128]{1,0:T(8,128)}, u32[]{:S(2)}) %copy-start) | copy-done | bytes 491544
  33.1 0.8 %copy.16 = f32[960,128]{1,0:T(8,128)} copy(f32[960,128]{1,0:T(8,128)S(1)} %copy-done) | data formatting | bytes 983040
Async XLA Ops:
  30.0 1.9 %copy-start.1 = (f32[960,128]{1,0:T(8,128)S(1)}, f32[960,128]{1,0:T(8,128)}, u32[]{:S(2)}) copy-start(f32[960,128]{1,0:T(8,128)} %get-tuple-element.7) | copy-start | bytes 1474564
  31.9 1.2 %copy-start = (f32[960,128]{1,0:T(8,128)S(1)}, f32[960,128]{1,0:T(8,128)}, u32[]{:S(2)}) copy-start(f32[960,128]{1,0:T(8,128)} %get-tuple-element.8) | copy-start | bytes 1474564

commit v3 on v2

--- a/solution.py
+++ b/solution.py
@@ -22,6 +22,7 @@
 epsilon = 1e-06
 MESH = pl.DeviceIdType.MESH
 OFFSETS = (-2, -1, 1, 2)
+BATCHES = ((2, 3, 4), (0, 1))
 UNROLL = 64
 
 
@@ -94,7 +95,7 @@
     sid_hbm, resp_hbm, sig_hbm, noise_hbm, lag_hbm, dir_hbm, res_hbm, est_hbm,
     sol_out, res_out, dir_out,
     sid_ref, resp_ref, sig_ref, noise_ref, lag_ref, dir_ref, res_ref, est_ref,
-    asend, abuf, fsend, fbuf, gsend, gbuf, vh_ref, vl_ref, psend, pbuf, esend, ebuf,
+    asend, abuf, fsend, fbuf, gsend, gbuf, vh_refs, vl_refs, image_ref, psend, pbuf, esend, ebuf,
     in_s, a_ss, a_rs, b_ss, b_rs, c_ss, c_rs, p_ss, p_rs, e_ss, e_rs,
 ):
     me = lax.axis_index("ra")
@@ -114,7 +115,8 @@
 
     def each_peer(action):
         if everyone <= UNROLL:
-            for i in range(1, everyone):
+            order = sorted(range(1, everyone), key=lambda i: min(i // m, n - i // m))
+            for i in order:
                 action(i)
         else:
             @pl.loop(1, everyone)
@@ -182,59 +184,60 @@
     for cp in loads[6:]:
         cp.wait()
     noise = jnp.concatenate([noise_ref[...], noise_ref[...]], axis=0)
-    for cp in a_copies:
-        cp.wait_recv()
-
-    rows = 10 * seg
-    weight = jnp.concatenate([abuf[g, 0 : 2 * seg, :] for g in range(5)], axis=0)
-    sid = jnp.concatenate([abuf[g, 2 * seg : 4 * seg, :] for g in range(5)], axis=0)
-    sin_h, cos_h = sincos_turns(ra_turns - sid * (1.0 / TWO_PI))
-    delay = cos_dec * (baseline_x * cos_h + baseline_y * sin_h) + baseline_z * sin_dec
-    row_id = lax.broadcasted_iota(jnp.int32, (rows, pix), 0)
-    shift = jnp.where(lax.rem(row_id, 2 * seg) >= seg, 0.25, 0.0)
-    half = bin_width * (SPAN - 1) / 2
-    fine = [sincos_turns((half * float(nodes[r])) * delay) for r in range(count // 2)]
-
-    b_copies = []
-    for index, (k0, k1) in enumerate(chunks):
-        centre = low_freq + bin_width * (
-            (band * bins + k0).astype(jnp.float32) + (SPAN - 1) / 2
-        )
-        p = reduce_turns(centre * delay)
-        t0 = weight * cos_turns(p - shift)
-        t1 = weight * cos_turns(p - shift + 0.25)
-        up, down = [], []
-        for sin_d, cos_d in fine:
-            a, b = t0 * cos_d, t1 * sin_d
-            up.append(a + b)
-            down.append(a - b)
-        table = jnp.concatenate(up + down[::-1], axis=0)
-        vh, vl = split(table)
-        vh_ref[index] = vh
-        vl_ref[index] = vl
-        product = lax.dot_general(
-            jnp.concatenate([vh, vl, vh], axis=1), dcat[k0:k1],
-            (((1,), (1,)), ((), ())), preferred_element_type=jnp.float32,
-        )
-        total = lag_ref[0:1, 0 : k1 - k0] * product[0:rows]
-        for r in range(1, count):
-            total = total + lag_ref[r : r + 1, 0 : k1 - k0] * product[r * rows : (r + 1) * rows]
-        for g in range(5):
-            fsend[index, g, :, 0 : k1 - k0] = total[g * 2 * seg : (g + 1) * 2 * seg]
-        for d in OFFSETS:
-            g = d + 2
-            cp = remote(
-                fsend.at[index, g], fbuf.at[index, g],
-                b_ss.at[index, g], b_rs.at[index, g], {"ra": ra_of(-d)},
-            )
-            cp.start()
-            b_copies.append(cp)
-
-    c_copies = []
+    b_copies = {}
+    for batch, groups in enumerate(BATCHES):
+        for g in groups:
+            if g != 2:
+                a_copies[OFFSETS.index(g - 2)].wait_recv()
+        rows = len(groups) * 2 * seg
+        weight = jnp.concatenate([abuf[g, 0 : 2 * seg, :] for g in groups], axis=0)
+        sid = jnp.concatenate([abuf[g, 2 * seg : 4 * seg, :] for g in groups], axis=0)
+        sin_h, cos_h = sincos_turns(ra_turns - sid * (1.0 / TWO_PI))
+        delay = cos_dec * (baseline_x * cos_h + baseline_y * sin_h) + baseline_z * sin_dec
+        row_id = lax.broadcasted_iota(jnp.int32, (rows, pix), 0)
+        shift = jnp.where(lax.rem(row_id, 2 * seg) >= seg, 0.25, 0.0)
+        half = bin_width * (SPAN - 1) / 2
+        fine = [sincos_turns((half * float(nodes[r])) * delay) for r in range(count // 2)]
+        for index, (k0, k1) in enumerate(chunks):
+            centre = low_freq + bin_width * (
+                (band * bins + k0).astype(jnp.float32) + (SPAN - 1) / 2
+            )
+            p = reduce_turns(centre * delay)
+            t0 = weight * cos_turns(p - shift)
+            t1 = weight * cos_turns(p - shift + 0.25)
+            up, down = [], []
+            for sin_d, cos_d in fine:
+                a, b = t0 * cos_d, t1 * sin_d
+                up.append(a + b)
+                down.append(a - b)
+            table = jnp.concatenate(up + down[::-1], axis=0)
+            vh, vl = split(table)
+            vh_refs[batch][index] = vh
+            vl_refs[batch][index] = vl
+            product = lax.dot_general(
+                jnp.concatenate([vh, vl, vh], axis=1), dcat[k0:k1],
+                (((1,), (1,)), ((), ())), preferred_element_type=jnp.float32,
+            )
+            total = lag_ref[0:1, 0 : k1 - k0] * product[0:rows]
+            for r in range(1, count):
+                total = total + (
+                    lag_ref[r : r + 1, 0 : k1 - k0] * product[r * rows : (r + 1) * rows]
+                )
+            for at, g in enumerate(groups):
+                fsend[index, g, :, 0 : k1 - k0] = total[at * 2 * seg : (at + 1) * 2 * seg]
+                if g != 2:
+                    cp = remote(
+                        fsend.at[index, g], fbuf.at[index, g],
+                        b_ss.at[index, g], b_rs.at[index, g], {"ra": ra_of(2 - g)},
+                    )
+                    cp.start()
+                    b_copies[index, g] = cp
+
+    c_copies = {}
     power = jnp.zeros((1, pix), jnp.float32)
     for index, (k0, k1) in enumerate(chunks):
-        for cp in b_copies[index * 4 : index * 4 + 4]:
-            cp.wait_recv()
+        for d in OFFSETS:
+            b_copies[index, d + 2].wait_recv()
         forward = fsend[index, 2, :, 0 : k1 - k0]
         for d in OFFSETS:
             forward = forward + fbuf[index, d + 2, :, 0 : k1 - k0]
@@ -247,7 +250,7 @@
                 c_ss.at[index, g], c_rs.at[index, g], {"ra": ra_of(d)},
             )
             cp.start()
-            c_copies.append(cp)
+            c_copies[index, g] = cp
         gbuf[index, 2, :, 0 : k1 - k0] = weighted
         both = jnp.sum(weighted * forward, axis=0, keepdims=True)
         for q in range(0, k1 - k0, pix):
@@ -273,37 +276,49 @@
     pbuf[0] = psend[...]
     share(psend, pbuf, p_ss, p_rs)
 
-    images = []
-    for index, (k0, k1) in enumerate(chunks):
-        for cp in c_copies[index * 4 : index * 4 + 4]:
-            cp.wait_recv()
-        g = jnp.concatenate([gbuf[index, j, :, 0 : k1 - k0] for j in range(5)], axis=0)
-        spread = jnp.concatenate(
-            [lag_ref[r : r + 1, 0 : k1 - k0] * g for r in range(count)], axis=0
-        )
-        gh, gl = split(spread)
-        vh, vl = vh_ref[index], vl_ref[index]
-        image_t = lax.dot_general(
-            jnp.concatenate([vh, vl, vh], axis=0), jnp.concatenate([gh, gh, gl], axis=0),
-            (((0,), (0,)), ((), ())), preferred_element_type=jnp.float32,
-        )
-        res_out[k0:k1, :] = image_t.T
-
+    cross = jnp.zeros((1, pix), jnp.float32)
+    norm = jnp.zeros((1, pix), jnp.float32)
+    for batch, groups in enumerate(BATCHES):
+        for index, (k0, k1) in enumerate(chunks):
+            for j in groups:
+                if j != 2:
+                    c_copies[index, j].wait_recv()
+            g = jnp.concatenate([gbuf[index, j, :, 0 : k1 - k0] for j in groups], axis=0)
+            spread = jnp.concatenate(
+                [lag_ref[r : r + 1, 0 : k1 - k0] * g for r in range(count)], axis=0
+            )
+            gh, gl = split(spread)
+            vh, vl = vh_refs[batch][index], vl_refs[batch][index]
+            image_t = lax.dot_general(
+                jnp.concatenate([vh, vl, vh], axis=0), jnp.concatenate([gh, gh, gl], axis=0),
+                (((0,), (0,)), ((), ())), preferred_element_type=jnp.float32,
+            )
+            if batch == 0:
+                image_ref[k0:k1, :] = image_t.T
+            else:
+                image = image_ref[k0:k1, :] + image_t.T
+                image_ref[k0:k1, :] = image
+                cross = cross + jnp.sum(image * res_ref[k0:k1, :], axis=0, keepdims=True)
+                norm = norm + jnp.sum(image * image, axis=0, keepdims=True)
+
+    esend[0:1, 0:pix] = cross
+    esend[0:1, pix : 2 * pix] = norm
+    ebuf[0] = esend[...]
+    share(esend, ebuf, e_ss, e_rs)
     totals = gathered(psend, pbuf, p_ss, p_rs)
-    rr_all = jnp.sum(totals[:, 0:pix], axis=1, keepdims=True) + epsilon
-    alpha = rr_all / (jnp.sum(totals[:, pix : 2 * pix], axis=1, keepdims=True) + epsilon)
-    residual_next = res_ref[...] - alpha * res_out[...]
-    res_out[...] = residual_next
-    norm = jnp.sum(residual_next * residual_next, axis=0, keepdims=True)
-    esend[...] = norm
-    ebuf[0] = norm
-    share(esend, ebuf, e_ss, e_rs)
+    rr_all = jnp.sum(totals[:, 0:pix], axis=1, keepdims=True)
+    power_all = jnp.sum(totals[:, pix : 2 * pix], axis=1, keepdims=True)
+    alpha = (rr_all + epsilon) / (power_all + epsilon)
     sol_out[...] = est_ref[...] + alpha * dir_ref[...]
-    for cp in a_copies + b_copies + c_copies:
+    res_out[...] = res_ref[...] - alpha * image_ref[...]
+    for cp in a_copies + list(b_copies.values()) + list(c_copies.values()):
         cp.wait_send()
     sent(psend, pbuf, p_ss, p_rs)
-    norm_all = jnp.sum(gathered(esend, ebuf, e_ss, e_rs), axis=1, keepdims=True)
-    beta = norm_all / rr_all
+    totals = gathered(esend, ebuf, e_ss, e_rs)
+    cross_all = jnp.sum(totals[:, 0:pix], axis=1, keepdims=True)
+    norm_all = jnp.sum(totals[:, pix : 2 * pix], axis=1, keepdims=True)
+    norm_next = rr_all - 2.0 * alpha * cross_all + alpha * alpha * norm_all
+    beta = norm_next / (rr_all + epsilon)
     dir_out[...] = res_out[...] + beta * dir_ref[...]
     sent(esend, ebuf, e_ss, e_rs)
 
@@ -324,9 +339,9 @@
             sidereal, response, significant, inv_noise, jnp.asarray(lagrange),
             direction, residual, estimate,
         )
-        return pl.pallas_call(
+        updated = pl.pallas_call(
             functools.partial(kernel, n, m, nodes),
-            out_shape=(jax.ShapeDtypeStruct((bins, pix), f32),) * 3,
+            out_shape=(pltpu.VMEM((bins, pix), f32),) * 3,
             in_specs=[pl.BlockSpec(memory_space=pl.ANY)] * len(operands),
             out_specs=(vmem,) * 3,
             scratch_shapes=[pltpu.SMEM(sidereal.shape, f32)]
@@ -338,12 +353,13 @@
                 pltpu.VMEM((pieces, 5, 2 * seg, SPAN), f32),
                 pltpu.VMEM((pieces, 2 * seg, SPAN), f32),
                 pltpu.VMEM((pieces, 5, 2 * seg, SPAN), f32),
-                pltpu.VMEM((pieces, count * 10 * seg, pix), bf16),
-                pltpu.VMEM((pieces, count * 10 * seg, pix), bf16),
+                [pltpu.VMEM((pieces, count * 2 * seg * len(b), pix), bf16) for b in BATCHES],
+                [pltpu.VMEM((pieces, count * 2 * seg * len(b), pix), bf16) for b in BATCHES],
+                pltpu.VMEM((bins, pix), f32),
                 pltpu.VMEM((1, 2 * pix), f32),
                 pltpu.VMEM((n * m, 1, 2 * pix), f32),
-                pltpu.VMEM((1, pix), f32),
-                pltpu.VMEM((n * m, 1, pix), f32),
+                pltpu.VMEM((1, 2 * pix), f32),
+                pltpu.VMEM((n * m, 1, 2 * pix), f32),
                 dma((len(operands),)),
             ]
             + [dma((5,))] * 2
@@ -351,6 +367,7 @@
             + [dma((n * m,))] * 4,
             compiler_params=pltpu.CompilerParams(collective_id=0, has_side_effects=True),
         )(*operands)
+        return updated
 
     return jax.shard_map(
         shards,

time: 34.1 us -> 30.4 us (0.89)
  Pallas kernels: 29.3 us -> 27.2 us
  local copies, waits for them, and re-layouts: 3.89 us -> 2.34 us
    pallas_call x1, Pallas kernels: 29.3 us -> 27.2 us  [shards(): pl.pallas_call(functools.partial(kernel, n, m, nodes), out_shape=(pltpu.V...]
    unnamed x7 -> x3, local copies, waits for them, and re-layouts: 3.89 us -> 2.34 us
where the time goes in v3:
time: 30.4 us; the launch traced here: 30.2 us
  Pallas kernels  27.2 us (89%)
  local copies, waits for them, and re-layouts  2.34 us (8%)
  between operations  0.64 us (2%)
    pallas_call x1, Pallas kernels, shards(): pl.pallas_call(functools.partial(kernel, n, m, nodes), out_shape=(pltpu.V...  27.2 us
    unnamed x3, local copies, waits for them, and re-layouts  2.34 us

profile of v3, /device:TPU:0, one launch (start us, length us, event | category | flops | bytes accessed | tf_op | source)
XLA Modules:
  0.0 30.2 jit_solution(15064039937502390932)
XLA Ops:
  0.6 27.2 %shard_map.103 = (f32[960,128]{1,0:T(8,128)S(1)}, f32[960,128]{1,0:T(8,128)S(1)}, f32[960,128]{1,0:T(8,128)S(1)}) custom-call(f32[4]{0:T(128)} %sid_hbm.1, f32[4,640]{1,0:T(4,128)} %resp_hbm.1, s32[4,10]{1,0:T(4,128)} %sig_hbm.1, f32[4,960]{1,0:T(4,128)} %noise_hbm.1, f32[12,256]{1,0:T(8,128)} %constant.2.clone.lag_hbm, f32[960,128]{1,0:T(8,128)} %dir_hbm.1, ...), custom_call_target="tpu_custom_call" | custom-call | tf_op jit(solution)/shard_map/pallas_call | solution.py:342
  27.9 0.8 %copy.14 = f32[960,128]{1,0:T(8,128)} copy(f32[960,128]{1,0:T(8,128)S(1)} %get-tuple-element.3) | data formatting | bytes 983040
  28.6 0.8 %copy.15 = f32[960,128]{1,0:T(8,128)} copy(f32[960,128]{1,0:T(8,128)S(1)} %get-tuple-element.4) | data formatting | bytes 983040
  29.4 0.8 %copy.16 = f32[960,128]{1,0:T(8,128)} copy(f32[960,128]{1,0:T(8,128)S(1)} %get-tuple-element.5) | data formatting | bytes 983040

commit v4 on v3

--- a/solution.py
+++ b/solution.py
@@ -279,10 +279,11 @@
     cross = jnp.zeros((1, pix), jnp.float32)
     norm = jnp.zeros((1, pix), jnp.float32)
     for batch, groups in enumerate(BATCHES):
-        for index, (k0, k1) in enumerate(chunks):
+        for index in range(len(chunks)):
             for j in groups:
                 if j != 2:
                     c_copies[index, j].wait_recv()
+        for index, (k0, k1) in enumerate(chunks):
             g = jnp.concatenate([gbuf[index, j, :, 0 : k1 - k0] for j in groups], axis=0)
             spread = jnp.concatenate(
                 [lag_ref[r : r + 1, 0 : k1 - k0] * g for r in range(count)], axis=0

time: 30.4 us -> 30 us (0.987)
  Pallas kernels: 27.2 us -> 26.8 us
    pallas_call x1, Pallas kernels: 27.2 us -> 26.8 us  [shards(): pl.pallas_call(functools.partial(kernel, n, m, nodes), out_shape=(pltpu.V...]
where the time goes in v4:
time: 30 us; the launch traced here: 29.8 us
  Pallas kernels  26.8 us (89%)
  local copies, waits for them, and re-layouts  2.34 us (8%)
  between operations  0.64 us (2%)
    pallas_call x1, Pallas kernels, shards(): pl.pallas_call(functools.partial(kernel, n, m, nodes), out_shape=(pltpu.V...  26.8 us
    unnamed x3, local copies, waits for them, and re-layouts  2.34 us

profile of v4, /device:TPU:0, one launch (start us, length us, event | category | flops | bytes accessed | tf_op | source)
XLA Modules:
  0.0 29.8 jit_solution(2164752292040140862)
XLA Ops:
  0.6 26.8 %shard_map.103 = (f32[960,128]{1,0:T(8,128)S(1)}, f32[960,128]{1,0:T(8,128)S(1)}, f32[960,128]{1,0:T(8,128)S(1)}) custom-call(f32[4]{0:T(128)} %sid_hbm.1, f32[4,640]{1,0:T(4,128)} %resp_hbm.1, s32[4,10]{1,0:T(4,128)} %sig_hbm.1, f32[4,960]{1,0:T(4,128)} %noise_hbm.1, f32[12,256]{1,0:T(8,128)} %constant.2.clone.lag_hbm, f32[960,128]{1,0:T(8,128)} %dir_hbm.1, ...), custom_call_target="tpu_custom_call" | custom-call | tf_op jit(solution)/shard_map/pallas_call | solution.py:343
  27.5 0.8 %copy.14 = f32[960,128]{1,0:T(8,128)} copy(f32[960,128]{1,0:T(8,128)S(1)} %get-tuple-element.3) | data formatting | bytes 983040
  28.2 0.8 %copy.15 = f32[960,128]{1,0:T(8,128)} copy(f32[960,128]{1,0:T(8,128)S(1)} %get-tuple-element.4) | data formatting | bytes 983040
  29.0 0.8 %copy.16 = f32[960,128]{1,0:T(8,128)} copy(f32[960,128]{1,0:T(8,128)S(1)} %get-tuple-element.5) | data formatting | bytes 983040
